TPU v7x, 32 devices: a whole 2x2x4 slice. The times are simulated.
32 devices in a mesh: fsdp: 4 (over z), ctx: 2 (over x), tp: 4 (over y, core).
Axes of the slice: x: 2, y: 2, z: 4, core: 2. Of those that a mesh axis runs over, the one named last changes fastest.
Arguments:
- tokens: bfloat16 [4, 2048, 2048], P('fsdp', 'ctx'), may hold values from -6 to 6
- segments: int32 [4, 2048], P('fsdp'), may hold values from 0 to 7, never falling along the last dimension, each value on 1 to 1024 neighbouring positions
- cotangent: bfloat16 [4, 2048, 2048], P('fsdp', 'ctx'), may hold values from -6 to 6
- gain_mix: float32 [2048], replicated, may hold values from 0.5 to 1.5
- w_branch: bfloat16 [2048, 2560], P('fsdp', 'tp'), may hold values from -0.125 to 0.125
- w_input: bfloat16 [2048, 2560], P('fsdp', 'tp'), may hold values from -0.125 to 0.125
- conv_weight: float32 [4, 2560], P(None, 'tp'), may hold values from -3 to 3
- conv_bias: float32 [2560], P('tp'), may hold values from -1.75 to 1.75
- gate_a: bfloat16 [16, 160, 160], P('tp'), may hold values from -0.5 to 0.5
- bias_a: float32 [2560], P('tp'), may hold values from -3 to 3
- gate_x: bfloat16 [16, 160, 160], P('tp'), may hold values from -0.5 to 0.5
- bias_x: float32 [2560], P('tp'), may hold values from -3 to 3
- decay_param: float32 [2560], P('tp'), may hold values from 4 to 8
- w_out: bfloat16 [2560, 2048], P('tp', 'fsdp'), may hold values from -0.3125 to 0.3125
- gain_mlp: float32 [2048], replicated, may hold values from 0.5 to 1.5
- w_gate: bfloat16 [2048, 6144], P('fsdp', 'tp'), may hold values from -0.125 to 0.125
- w_up: bfloat16 [2048, 6144], P('fsdp', 'tp'), may hold values from -0.125 to 0.125
- w_down: bfloat16 [6144, 2048], P('tp', 'fsdp'), may hold values from -0.15625 to 0.15625
Outputs:
- output: bfloat16 [4, 2048, 2048], P('fsdp', 'ctx')
- grad_tokens: bfloat16 [4, 2048, 2048], P('fsdp', 'ctx')
- grad_gain_mix: float32 [2048], replicated
- grad_w_branch: float32 [2048, 2560], P('fsdp', 'tp')
- grad_w_input: float32 [2048, 2560], P('fsdp', 'tp')
- grad_conv_weight: float32 [4, 2560], P(None, 'tp')
- grad_conv_bias: float32 [2560], P('tp')
- grad_gate_a: float32 [16, 160, 160], P('tp')
- grad_bias_a: float32 [2560], P('tp')
- grad_gate_x: float32 [16, 160, 160], P('tp')
- grad_bias_x: float32 [2560], P('tp')
- grad_decay_param: float32 [2560], P('tp')
- grad_w_out: float32 [2560, 2048], P('tp', 'fsdp')
- grad_gain_mlp: float32 [2048], replicated
- grad_w_gate: float32 [2048, 6144], P('fsdp', 'tp')
- grad_w_up: float32 [2048, 6144], P('fsdp', 'tp')
- grad_w_down: float32 [6144, 2048], P('tp', 'fsdp')
Inputs may be any that keep to these rules, and one draw needn't show every extreme that they name: `segments`: within a sequence the document numbers never fall; every document has 1 to 1024 positions and one has exactly 1024.
All inputs are finite; a program needn't handle non-finite values.
Results may differ from a plain program's by a relative error of at most 0.012.
Values may be sent and summed in bfloat16 or wider, within the bound.
A program may use at most 256 MiB of HBM per device.

v0:
```python
import jax
import jax.numpy as jnp
from jax import lax
from jax.sharding import PartitionSpec as P

EPSILON = 1e-06
RATE_SCALE = 8.0


def passed_along(block, axis, distance):
    devices = range(lax.axis_size(axis))
    route = [(i - distance, i) for i in devices if i - distance in devices]
    return lax.ppermute(block, axis, route)


def entering_2(x, axis, combine, identity, reverse):
    length, place = (lax.axis_size(axis), lax.axis_index(axis))
    everything = jax.tree.map(lambda part: lax.all_gather(part, axis), x)
    start = jax.tree.map(
        lambda part, zero: jnp.broadcast_to(jnp.asarray(zero, part.dtype), part.shape), x, identity
    )

    def turn(k, before):
        at = length - 1 - k if reverse else k
        reached = at > place if reverse else at < place
        new = combine(before, jax.tree.map(lambda part: part[at], everything))
        return jax.tree.map(lambda a, b: jnp.where(reached, a, b), new, before)

    return lax.fori_loop(0, length, turn, start)


def linear_combine(earlier, later):
    return (earlier[0] * later[0], later[0] * earlier[1] + later[1])


def matmul(left, right):
    return jnp.dot(left, right, preferred_element_type=jnp.float32)


def left_inner(left, right):
    return lax.dot_general(
        left, right, (((0,), (0,)), ((), ())), preferred_element_type=jnp.float32
    )


def right_inner(left, right):
    return lax.dot_general(
        left, right, (((1,), (1,)), ((), ())), preferred_element_type=jnp.float32
    )


def gelu_slope(values):
    result, pull_back = jax.vjp(lambda inner_v: jax.nn.gelu(inner_v, approximate=True), values)
    return (result, pull_back(jnp.ones_like(values))[0])


def rms_rows(values):
    return lax.rsqrt(jnp.mean(values * values, axis=-1, keepdims=True) + EPSILON)


def norm_back(grad_norm, scaled, scale_row, gain):
    grad_scaled = grad_norm * gain
    return scale_row * (
        grad_scaled - scaled * jnp.mean(grad_scaled * scaled, axis=-1, keepdims=True)
    )


def shards(
    tokens,
    segments,
    cotangent,
    gain_mix,
    w_branch,
    w_input,
    conv_weight,
    conv_bias,
    gate_a,
    bias_a,
    gate_x,
    bias_x,
    decay_param,
    w_out,
    gain_mlp,
    w_gate,
    w_up,
    w_down,
):
    full_branch, full_input, full_gate, full_up, full_out, full_down = (
        lax.all_gather(w_branch, "fsdp", axis=0, tiled=True),
        lax.all_gather(w_input, "fsdp", axis=0, tiled=True),
        lax.all_gather(w_gate, "fsdp", axis=0, tiled=True),
        lax.all_gather(w_up, "fsdp", axis=0, tiled=True),
        lax.all_gather(w_out, "fsdp", axis=1, tiled=True),
        lax.all_gather(w_down, "fsdp", axis=1, tiled=True),
    )
    seq_count, tok_count, model_width = tokens.shape
    row_count = seq_count * tok_count
    kernel = conv_weight.shape[0]
    lag_rows = kernel - 1
    local_width = conv_bias.shape[0]
    head_count = gate_a.shape[0]
    block_width = gate_a.shape[1]
    inputs = tokens.reshape(row_count, model_width).astype(jnp.float32)
    scale_mix = rms_rows(inputs)
    scaled_mix = inputs * scale_mix
    normed = (scaled_mix * gain_mix).astype(jnp.bfloat16)
    branch_pre = matmul(normed, full_branch)
    branch, branch_slope = gelu_slope(branch_pre)
    conv_in = (
        matmul(normed, full_input).astype(jnp.bfloat16).reshape(seq_count, tok_count, local_width)
    )
    first_pos = lax.axis_index("ctx") * tok_count
    padded_seg = jnp.pad(segments, ((0, 0), (lag_rows, lag_rows)), constant_values=-1)
    near_seg = lax.dynamic_slice_in_dim(padded_seg, first_pos, tok_count + 2 * lag_rows, 1)
    own_seg = near_seg[:, lag_rows : lag_rows + tok_count]
    same_back = [
        near_seg[:, lag_rows - offset : lag_rows - offset + tok_count] == own_seg
        for offset in range(kernel)
    ]
    same_ahead = [
        near_seg[:, lag_rows + offset : lag_rows + offset + tok_count] == own_seg
        for offset in range(kernel)
    ]
    tail_rows = passed_along(conv_in[:, tok_count - lag_rows :], "ctx", 1)
    conv_ext = jnp.concatenate([tail_rows, conv_in], axis=1)
    conv_sum = jnp.zeros((seq_count, tok_count, local_width), jnp.float32) + conv_bias
    for offset in range(kernel):
        earlier_in = jnp.where(
            same_back[offset][..., None],
            conv_ext[:, lag_rows - offset : lag_rows - offset + tok_count],
            0.0,
        )
        conv_sum = conv_sum + conv_weight[offset] * earlier_in
    conv_out = conv_sum.astype(jnp.bfloat16)
    conv_heads = conv_out.reshape(seq_count, tok_count, head_count, block_width)
    pre_a = (
        jnp.einsum(
            "sthi,hij->sthj", conv_heads, gate_a, preferred_element_type=jnp.float32
        ).reshape(seq_count, tok_count, local_width)
        + bias_a
    )
    pre_x = (
        jnp.einsum(
            "sthi,hij->sthj", conv_heads, gate_x, preferred_element_type=jnp.float32
        ).reshape(seq_count, tok_count, local_width)
        + bias_x
    )
    recur_gate = jax.nn.sigmoid(pre_a)
    input_gate = jax.nn.sigmoid(pre_x)
    softened = jax.nn.softplus(-decay_param)
    log_decay = -RATE_SCALE * softened * recur_gate
    decay = jnp.exp(log_decay)
    root_term = jnp.sqrt(-jnp.expm1(2.0 * log_decay))
    starts = jnp.logical_not(same_back[1])[..., None]
    multiplier = jnp.where(starts, 1.0, root_term)
    carry_factor = jnp.where(starts, 0.0, decay)
    conv_float = conv_out.astype(jnp.float32)
    driven = input_gate * conv_float * multiplier
    decay_run, local_states = lax.associative_scan(linear_combine, (carry_factor, driven), axis=1)
    ones_state = jnp.ones((seq_count, local_width), jnp.float32)
    zero_state = jnp.zeros((seq_count, local_width), jnp.float32)
    entering = entering_2(
        (decay_run[:, -1], local_states[:, -1]),
        "ctx",
        linear_combine,
        (ones_state, zero_state),
        False,
    )[1]
    states = local_states + decay_run * entering[:, None]
    states_rows = states.reshape(row_count, local_width)
    mixed_out = (states_rows * branch).astype(jnp.bfloat16)
    mixer_term = matmul(mixed_out, full_out)
    resid_rows = inputs + lax.psum(mixer_term, "tp")
    scale_mlp = rms_rows(resid_rows)
    scaled_mlp = resid_rows * scale_mlp
    normed_mlp = (scaled_mlp * gain_mlp).astype(jnp.bfloat16)
    gate_pre = matmul(normed_mlp, full_gate)
    up_pre = matmul(normed_mlp, full_up)
    gate_act, gate_slope = gelu_slope(gate_pre)
    hidden = (gate_act * up_pre).astype(jnp.bfloat16)
    down_term = matmul(hidden, full_down)
    output = (resid_rows + lax.psum(down_term, "tp")).astype(jnp.bfloat16)
    grad_low = cotangent.reshape(row_count, model_width)
    grad_out = grad_low.astype(jnp.float32)
    grad_w_down = left_inner(hidden, grad_low)
    grad_hidden = right_inner(grad_low, full_down)
    grad_gate = (grad_hidden * up_pre * gate_slope).astype(jnp.bfloat16)
    grad_up = (grad_hidden * gate_act).astype(jnp.bfloat16)
    grad_w_gate = left_inner(normed_mlp, grad_gate)
    grad_w_up = left_inner(normed_mlp, grad_up)
    mlp_back_term = right_inner(grad_gate, full_gate) + right_inner(grad_up, full_up)
    grad_norm_mlp = lax.psum(mlp_back_term, "tp")
    grad_resid = grad_out + norm_back(grad_norm_mlp, scaled_mlp, scale_mlp, gain_mlp)
    grad_proj = grad_resid.astype(jnp.bfloat16)
    grad_gain_mlp = jnp.sum(grad_norm_mlp * scaled_mlp, axis=0)
    grad_w_out = left_inner(mixed_out, grad_proj)
    grad_mixed = right_inner(grad_proj, full_out)
    grad_branch = (grad_mixed * states_rows * branch_slope).astype(jnp.bfloat16)
    grad_states = (grad_mixed * branch).reshape(seq_count, tok_count, local_width)
    next_factor = jnp.concatenate(
        [carry_factor[:, 1:], jnp.ones((seq_count, 1, local_width), jnp.float32)], axis=1
    )
    run_back, local_back = lax.associative_scan(
        linear_combine, (jnp.flip(next_factor, 1), jnp.flip(grad_states, 1)), axis=1
    )
    run_back = jnp.flip(run_back, 1)
    local_back = jnp.flip(local_back, 1)
    leaving = (carry_factor[:, 0] * run_back[:, 0], carry_factor[:, 0] * local_back[:, 0])
    arriving = entering_2(leaving, "ctx", linear_combine, (ones_state, zero_state), True)[1]
    grad_total = local_back + run_back * arriving[:, None]
    prev_states = jnp.concatenate([entering[:, None], states[:, :-1]], axis=1)
    grad_mult = grad_total * input_gate * conv_float
    grad_log = jnp.where(
        starts, 0.0, grad_total * prev_states * decay - grad_mult * decay * decay / root_term
    )
    grad_decay_param = (
        RATE_SCALE * jax.nn.sigmoid(-decay_param) * jnp.sum(grad_log * recur_gate, axis=(0, 1))
    )
    grad_pre_a = (grad_log * (-RATE_SCALE * softened) * recur_gate * (1.0 - recur_gate)).astype(
        jnp.bfloat16
    )
    grad_pre_x = (grad_total * conv_float * multiplier * input_gate * (1.0 - input_gate)).astype(
        jnp.bfloat16
    )
    heads_a = grad_pre_a.reshape(seq_count, tok_count, head_count, block_width)
    heads_x = grad_pre_x.reshape(seq_count, tok_count, head_count, block_width)
    grad_gate_a = jnp.einsum(
        "sthi,sthj->hij", conv_heads, heads_a, preferred_element_type=jnp.float32
    )
    grad_gate_x = jnp.einsum(
        "sthi,sthj->hij", conv_heads, heads_x, preferred_element_type=jnp.float32
    )
    grad_bias_a = jnp.sum(grad_pre_a.astype(jnp.float32), axis=(0, 1))
    grad_bias_x = jnp.sum(grad_pre_x.astype(jnp.float32), axis=(0, 1))
    gate_back = jnp.einsum(
        "sthj,hij->sthi", heads_a, gate_a, preferred_element_type=jnp.float32
    ) + jnp.einsum("sthj,hij->sthi", heads_x, gate_x, preferred_element_type=jnp.float32)
    grad_conv = grad_total * input_gate * multiplier + gate_back.reshape(
        seq_count, tok_count, local_width
    )
    head_rows = passed_along(grad_conv[:, :lag_rows], "ctx", -1)
    grad_ext = jnp.concatenate([grad_conv, head_rows], axis=1)
    grad_conv_in = jnp.zeros((seq_count, tok_count, local_width), jnp.float32)
    weight_rows = []
    for offset in range(kernel):
        later_grad = jnp.where(
            same_ahead[offset][..., None], grad_ext[:, offset : offset + tok_count], 0.0
        )
        grad_conv_in = grad_conv_in + conv_weight[offset] * later_grad
        earlier_in = jnp.where(
            same_back[offset][..., None],
            conv_ext[:, lag_rows - offset : lag_rows - offset + tok_count],
            0.0,
        )
        weight_rows.append(jnp.sum(grad_conv * earlier_in, axis=(0, 1)))
    grad_conv_weight = jnp.stack(weight_rows)
    grad_conv_bias = jnp.sum(grad_conv, axis=(0, 1))
    grad_in_low = grad_conv_in.astype(jnp.bfloat16).reshape(row_count, local_width)
    grad_w_input = left_inner(normed, grad_in_low)
    grad_w_branch = left_inner(normed, grad_branch)
    mix_back_term = right_inner(grad_in_low, full_input) + right_inner(grad_branch, full_branch)
    grad_norm_mix = lax.psum(mix_back_term, "tp")
    grad_gain_mix = jnp.sum(grad_norm_mix * scaled_mix, axis=0)
    grad_tokens = (grad_resid + norm_back(grad_norm_mix, scaled_mix, scale_mix, gain_mix)).astype(
        jnp.bfloat16
    )
    owned = (
        lax.psum_scatter(grad_w_branch, "fsdp", scatter_dimension=0, tiled=True),
        lax.psum_scatter(grad_w_input, "fsdp", scatter_dimension=0, tiled=True),
        lax.psum_scatter(grad_w_gate, "fsdp", scatter_dimension=0, tiled=True),
        lax.psum_scatter(grad_w_up, "fsdp", scatter_dimension=0, tiled=True),
        lax.psum_scatter(grad_w_out, "fsdp", scatter_dimension=1, tiled=True),
        lax.psum_scatter(grad_w_down, "fsdp", scatter_dimension=1, tiled=True),
    )
    owned_branch, owned_input, owned_gate, owned_up, owned_out, owned_down = owned
    summed = lax.psum(
        (owned_branch, owned_input, owned_gate, owned_up, owned_out, owned_down), "ctx"
    )
    sum_branch, sum_input, sum_gate, sum_up, sum_out, sum_down = summed
    small_sums = lax.psum(
        (
            grad_gain_mix,
            grad_gain_mlp,
            grad_conv_weight,
            grad_conv_bias,
            grad_gate_a,
            grad_bias_a,
            grad_gate_x,
            grad_bias_x,
            grad_decay_param,
        ),
        ("fsdp", "ctx"),
    )
    (
        sum_gain_mix,
        sum_gain_mlp,
        sum_conv_weight,
        sum_conv_bias,
        sum_gate_a,
        sum_bias_a,
        sum_gate_x,
        sum_bias_x,
        sum_decay,
    ) = small_sums
    return (
        output.reshape(seq_count, tok_count, model_width),
        grad_tokens.reshape(seq_count, tok_count, model_width),
        sum_gain_mix,
        sum_branch,
        sum_input,
        sum_conv_weight,
        sum_conv_bias,
        sum_gate_a,
        sum_bias_a,
        sum_gate_x,
        sum_bias_x,
        sum_decay,
        sum_out,
        sum_gain_mlp,
        sum_gate,
        sum_up,
        sum_down,
    )


def solution(mesh):
    in_specs = (
        P("fsdp", "ctx", None),
        P("fsdp", None),
        P("fsdp", "ctx", None),
        P(),
        P("fsdp", "tp"),
        P("fsdp", "tp"),
        P(None, "tp"),
        P("tp"),
        P("tp", None, None),
        P("tp"),
        P("tp", None, None),
        P("tp"),
        P("tp"),
        P("tp", "fsdp"),
        P(),
        P("fsdp", "tp"),
        P("fsdp", "tp"),
        P("tp", "fsdp"),
    )
    out_specs = (
        P("fsdp", "ctx", None),
        P("fsdp", "ctx", None),
        P(),
        P("fsdp", "tp"),
        P("fsdp", "tp"),
        P(None, "tp"),
        P("tp"),
        P("tp", None, None),
        P("tp"),
        P("tp", None, None),
        P("tp"),
        P("tp"),
        P("tp", "fsdp"),
        P(),
        P("fsdp", "tp"),
        P("fsdp", "tp"),
        P("tp", "fsdp"),
    )
    return jax.shard_map(shards, mesh=mesh, in_specs=in_specs, out_specs=out_specs, check_vma=False)
```

profile of v0, /device:TPU:0, one launch (start us, length us, event | category | flops | bytes accessed | tf_op | source)
XLA Modules:
  0.0 3015.9 jit_solution(510944161602865288)
XLA Ops:
  13.5 53.5 %all-gather.7.cloned.1.call-done = bf16[2048,640]{1,0:T(8,128)(2,1)} async-done(((bf16[512,640]{1,0:T(8,128)(2,1)}), bf16[2048,640]{1,0:T(8,128)(2,1)}) %all-gather.7.cloned.1.call-update) | async-done | bytes 2621456 | tf_op jit(solution)/shard_map/all_gather | solution.py:90
  67.1 6.5 convolution_convert_fusion
  94.0 6.6 fusion.65
  100.6 7.1 slice.691
  107.7 7.0 slice.692
  243.0 7.1 slice.762
  327.9 9.0 pad.269
  336.9 9.0 pad.270
  348.4 9.0 pad.289
  357.5 9.0 pad.290
  377.1 12.8 fusion.76
  390.0 8.9 fusion.138
  400.8 150.4 %all-reduce.93.cloned.1.call-done = f32[1024,2048]{1,0:T(8,128)} async-done(((f32[1024,2048]{1,0:T(8,128)}), f32[1024,2048]{1,0:T(8,128)}) %all-reduce.93.cloned.1.call-update) | async-done | bytes 8388624 | tf_op jit(solution)/shard_map/psum | solution.py:173
  551.2 5.7 multiply_reduce_fusion.2
  563.1 105.0 %all-gather.13.cloned.1.call-done = bf16[2048,1536]{1,0:T(8,128)(2,1)} async-done(((bf16[512,1536]{1,0:T(8,128)(2,1)}), bf16[2048,1536]{1,0:T(8,128)(2,1)}) %all-gather.13.cloned.1.call-update) | async-done | bytes 6291472 | tf_op jit(solution)/shard_map/all_gather | solution.py:91
  668.1 12.2 fusion.139
  680.3 102.8 %all-gather.15.cloned.1.call-done = bf16[2048,1536]{1,0:T(8,128)(2,1)} async-done(((bf16[512,1536]{1,0:T(8,128)(2,1)}), bf16[2048,1536]{1,0:T(8,128)(2,1)}) %all-gather.15.cloned.1.call-update) | async-done | bytes 6291472 | tf_op jit(solution)/shard_map/all_gather | solution.py:92
  783.1 11.7 fusion.140
  794.8 103.4 %all-gather.17.cloned.1.call-done = bf16[1536,2048]{1,0:T(8,128)(2,1)} async-done(((bf16[1536,512]{1,0:T(8,128)(2,1)}), bf16[1536,2048]{1,0:T(8,128)(2,1)}) %all-gather.17.cloned.1.call-update) | async-done | bytes 6291472 | tf_op jit(solution)/shard_map/all_gather | solution.py:94
  898.2 18.2 multiply_convert_fusion.1
  916.5 10.0 fusion.142
  926.5 10.7 convolution_add_fusion.1
  937.2 151.2 %all-reduce.95.cloned.1.call-done = f32[1024,2048]{1,0:T(8,128)} async-done(((f32[1024,2048]{1,0:T(8,128)}), f32[1024,2048]{1,0:T(8,128)}) %all-reduce.95.cloned.1.call-update) | async-done | bytes 8388624 | tf_op jit(solution)/shard_map/psum | solution.py:192
  1088.4 7.6 multiply_reduce_fusion
  1112.3 7.1 slice.788
  1119.5 7.0 slice.793
  1126.5 7.0 slice.786
  1133.4 10.7 slice.789
  1144.2 10.7 slice.794
  1154.9 11.1 slice.787
  1166.0 12.5 fusion.54
  1178.4 20.8 reverse.9
  1199.2 7.0 slice.790
  1206.2 7.0 slice.791
  1325.2 7.0 slice.862
  1333.4 8.7 fusion.115
  1389.5 4.9 pad.327
  1402.3 9.2 pad.330
  1418.5 4.9 pad.308
  1426.3 9.3 pad.310
  1441.6 9.2 pad.309
  1453.3 9.2 pad.329
  1478.5 20.8 rev.13
  1499.3 20.9 rev.12
  1520.3 7.1 multiply_reduce_fusion.3
  1527.4 5.4 convert_reduce_fusion
  1545.1 8.9 fusion.44
  1563.2 5.6 fusion.27
  1568.8 12.6 fusion.145
  1581.6 12.5 fusion.146
  1594.1 12.2 fusion.30
  1606.4 12.1 fusion.141
  1622.0 5.9 convolution_add_fusion
  1632.6 29.5 reduce-scatter.9.cloned.1.call-done
  1662.1 214.6 %reduce-scatter.13.cloned.1.call-done = f32[512,1536]{1,0:T(8,128)} async-done(((f32[2048,1536]{1,0:T(8,128)}), f32[512,1536]{1,0:T(8,128)}) %reduce-scatter.13.cloned.1.call-update) | async-done | bytes 3145744 | tf_op jit(solution)/shard_map/reduce_scatter | solution.py:270
  1876.7 215.3 %reduce-scatter.15.cloned.1.call-done = f32[512,1536]{1,0:T(8,128)} async-done(((f32[2048,1536]{1,0:T(8,128)}), f32[512,1536]{1,0:T(8,128)}) %reduce-scatter.15.cloned.1.call-update) | async-done | bytes 3145744 | tf_op jit(solution)/shard_map/reduce_scatter | solution.py:271
  2092.0 215.2 %reduce-scatter.17.cloned.1.call-done = f32[1536,512]{1,0:T(8,128)} async-done(((f32[1536,2048]{1,0:T(8,128)}), f32[1536,512]{1,0:T(8,128)}) %reduce-scatter.17.cloned.1.call-update) | async-done | bytes 3145744 | tf_op jit(solution)/shard_map/reduce_scatter | solution.py:273
  2307.9 291.2 %all-reduce.99.cloned.1.call-done = (f32[1024,2048]{1,0:T(8,128)}, f32[1024,2048]{1,0:T(8,128)}) async-done(((f32[1024,2048]{1,0:T(8,128)}, f32[1024,2048]{1,0:T(8,128)}), (f32[1024,2048]{1,0:T(8,128)}, f32[1024,2048]{1,0:T(8,128)})) %all-reduce.99.cloned.1.call-update) | async-done | bytes 16777232 | tf_op jit(solution)/shard_map/psum | solution.py:182
  2599.0 5.9 fusion.13
  2604.9 39.3 %all-reduce.83 = (f32[2048]{0:T(1024)}, f32[4,640]{1,0:T(4,128)}, f32[640]{0:T(1024)}, f32[640]{0:T(1024)}, f32[640]{0:T(1024)}, /*index=5*/f32[640]{0:T(1024)}, f32[2048]{0:T(1024)}) all-reduce(f32[2048]{0:T(1024)S(1)} %get-tuple-element.283, ...), channel_id=1, replica_groups=mesh['fsdp'=4,'ctx'=2,'tp'=4] {'fsdp','ctx'}, use_global_device_ids=true, to_apply=%region_13.14 | all-reduce | flops 9216 | bytes 73728 | tf_op jit(solution)/shard_map/psum | solution.py:280
  2644.2 9.4 fusion.25
  2653.6 8.7 fusion.29
  2662.3 25.7 all-reduce.97.cloned.1.call-done
  2688.0 307.0 %all-reduce.101.cloned.1.call-done = (f32[512,640]{1,0:T(8,128)}, f32[512,640]{1,0:T(8,128)}, f32[640,512]{1,0:T(8,128)}, f32[512,1536]{1,0:T(8,128)}, f32[512,1536]{1,0:T(8,128)}, /*index=5*/f32[1536,512]{1,0:T(8,128)}) async-done(((f32[512,640]{1,0:T(8,128)}, f32[512,640]{1,0:T(8,128)}, f32[640,512]{1,0:T(8,128)}, f32[512,1536]{1,0:T(8,128)}, f32[512,1536]{1,0:T(8,128)}, ...) | async-done | bytes 13369360 | tf_op jit(solution)/shard_map/psum | solution.py:276
  (688 shorter events, 516.0 us)
Async XLA Ops:
  7.2 79.2 %copy-start = (bf16[4,160,160]{2,1,0:T(8,128)(2,1)S(1)}, bf16[4,160,160]{2,1,0:T(8,128)(2,1)}, u32[]{:S(2)}) copy-start(bf16[4,160,160]{2,1,0:T(8,128)(2,1)} %param.30) | copy-start | bytes 614404
  7.2 59.9 %all-gather.7.cloned.1.call-start = ((), (), s32[]{:S(2)}) async-start(), calls=%async_computation.6 | async-start | bytes 3276800 | tf_op jit(solution)/shard_map/all_gather | solution.py:90
  7.9 369.2 %all-gather.9.cloned.1.call-start = ((), (), s32[]{:S(2)}) async-start(), calls=%async_computation.7 | async-start | bytes 3276800 | tf_op jit(solution)/shard_map/all_gather | solution.py:89
  8.7 58.4 %copy-start.85 = (f32[2048]{0:T(1024)S(1)}, f32[2048]{0:T(1024)}, u32[]{:S(2)}) copy-start(f32[2048]{0:T(1024)} %param.25) | copy-start | bytes 24580
  8.7 381.2 %all-gather.11.cloned.1.call-start = ((), (), s32[]{:S(2)}) async-start(), calls=%async_computation.8 | async-start | bytes 3276800 | tf_op jit(solution)/shard_map/all_gather | solution.py:93
  9.5 541.8 %all-reduce.93.cloned.1.call-start = ((), (), s32[]{:S(2)}) async-start(), calls=%async_computation.9 | async-start | bytes 16777216 | tf_op jit(solution)/shard_map/psum | solution.py:173
  12.7 65.6 %copy-start.76 = (f32[640]{0:T(1024)}, f32[640]{0:T(1024)S(1)}, u32[]{:S(2)}) copy-start(f32[640]{0:T(1024)S(1)} %get-tuple-element.290) | copy-start | bytes 7684
  12.7 65.6 %copy-start.78 = (f32[640]{0:T(1024)}, f32[640]{0:T(1024)S(1)}, u32[]{:S(2)}) copy-start(f32[640]{0:T(1024)S(1)} %get-tuple-element.291) | copy-start | bytes 7684
  12.7 65.6 %copy-start.80 = (f32[640]{0:T(1024)}, f32[640]{0:T(1024)S(1)}, u32[]{:S(2)}) copy-start(f32[640]{0:T(1024)S(1)} %get-tuple-element.292) | copy-start | bytes 7684
  12.7 65.6 %copy-start.82 = (f32[640]{0:T(1024)}, f32[640]{0:T(1024)S(1)}, u32[]{:S(2)}) copy-start(f32[640]{0:T(1024)S(1)} %get-tuple-element.293) | copy-start | bytes 7684
  12.7 81.2 %copy-start.60 = (f32[640]{0:T(1024)}, f32[640]{0:T(1024)S(1)}, u32[]{:S(2)}) copy-start(f32[640]{0:T(1024)S(1)} %fusion.106) | copy-start | bytes 7684
  13.5 64.8 %copy-start.129 = (pred[1024]{0:T(1024)(128)(4,1)}, pred[1024]{0:T(1024)(128)(4,1)S(1)}, u32[]{:S(2)}) copy-start(pred[1024]{0:T(1024)(128)(4,1)S(1)} %get-tuple-element.295) | copy-start | bytes 3076
  13.5 64.8 %copy-start.131 = (pred[1024]{0:T(1024)(128)(4,1)}, pred[1024]{0:T(1024)(128)(4,1)S(1)}, u32[]{:S(2)}) copy-start(pred[1024]{0:T(1024)(128)(4,1)S(1)} %get-tuple-element.296) | copy-start | bytes 3076
  13.5 64.8 %copy-start.134 = (f32[640]{0:T(1024)S(1)}, f32[640]{0:T(1024)}, u32[]{:S(2)}) copy-start(f32[640]{0:T(1024)} %param.29) | copy-start | bytes 7684
  73.6 4.7 collective-permute-start
  77.0 17.0 copy-start.89
  100.6 14.1 copy-start.13
  238.6 13.7 copy-start.63
  238.7 13.7 copy-start.118
  238.7 15.1 copy-start.56
  238.7 15.1 copy-start.57
  243.0 14.4 copy-start.53
  298.2 14.6 copy-start.104
  357.5 19.6 copy-start.86
  398.9 269.3 %all-gather.13.cloned.1.call-start = ((), (), s32[]{:S(2)}) async-start(), calls=%async_computation.10 | async-start | bytes 7864320 | tf_op jit(solution)/shard_map/all_gather | solution.py:91
  399.5 383.6 %all-gather.15.cloned.1.call-start = ((), (), s32[]{:S(2)}) async-start(), calls=%async_computation.11 | async-start | bytes 7864320 | tf_op jit(solution)/shard_map/all_gather | solution.py:92
  400.0 498.2 %all-gather.17.cloned.1.call-start = ((), (), s32[]{:S(2)}) async-start(), calls=%async_computation.12 | async-start | bytes 7864320 | tf_op jit(solution)/shard_map/all_gather | solution.py:94
  400.8 159.6 %copy-start.65 = (f32[2048]{0:T(1024)S(1)}, f32[2048]{0:T(1024)}, u32[]{:S(2)}) copy-start(f32[2048]{0:T(1024)} %param.36) | copy-start | bytes 24580
  400.8 687.6 %all-reduce.95.cloned.1.call-start = ((), (), s32[]{:S(2)}) async-start(), calls=%async_computation.13 | async-start | bytes 16777216 | tf_op jit(solution)/shard_map/psum | solution.py:192
  937.2 695.4 %reduce-scatter.11.cloned.1.call-start = ((), (), s32[]{:S(2)}) async-start(), calls=%async_computation.16 | async-start | bytes 6553600 | tf_op jit(solution)/shard_map/reduce_scatter | solution.py:272
  1110.4 522.2 %reduce-scatter.7.cloned.1.call-start = ((), (), s32[]{:S(2)}) async-start(), calls=%async_computation.14 | async-start | bytes 6553600 | tf_op jit(solution)/shard_map/reduce_scatter | solution.py:268
  1313.8 19.1 copy-start.95
  1313.8 19.1 copy-start.96
  1313.8 19.1 copy-start.97
  1313.8 19.1 copy-start.98
  1313.9 19.1 copy-start.70
  1313.9 19.1 copy-start.71
  1313.9 19.3 copy-start.72
  1313.9 19.3 copy-start.73
  1313.9 19.4 copy-start.119
  1313.9 19.4 copy-start.117
  1318.2 15.2 copy-start.87
  1342.2 319.9 %reduce-scatter.9.cloned.1.call-start = ((), (), s32[]{:S(2)}) async-start(), calls=%async_computation.15 | async-start | bytes 6553600 | tf_op jit(solution)/shard_map/reduce_scatter | solution.py:269
  1499.2 21.0 copy-start.6
  1499.2 21.0 copy-start.59
  1499.2 21.0 copy-start.61
  1499.2 21.0 copy-start.67
  1499.2 21.0 copy-start.69
  1499.3 21.0 copy-start.90
  1545.0 14.6 copy-start.77
  1545.0 14.6 copy-start.79
  1545.0 14.6 copy-start.81
  1545.1 14.6 copy-start.83
  1545.1 14.6 copy-start.135
  1545.1 14.6 copy-start.136
  1545.1 14.6 copy-start.137
  1545.1 18.1 copy-start.3
  1554.1 5.6 collective-permute-start.1
  1568.8 307.9 %reduce-scatter.13.cloned.1.call-start = ((), (), s32[]{:S(2)}) async-start(), calls=%async_computation.17 | async-start | bytes 15728640 | tf_op jit(solution)/shard_map/reduce_scatter | solution.py:270
  1581.5 510.5 %reduce-scatter.15.cloned.1.call-start = ((), (), s32[]{:S(2)}) async-start(), calls=%async_computation.18 | async-start | bytes 15728640 | tf_op jit(solution)/shard_map/reduce_scatter | solution.py:271
  1594.1 713.1 %reduce-scatter.17.cloned.1.call-start = ((), (), s32[]{:S(2)}) async-start(), calls=%async_computation.19 | async-start | bytes 15728640 | tf_op jit(solution)/shard_map/reduce_scatter | solution.py:273
  1606.4 992.6 %all-reduce.99.cloned.1.call-start = ((), (), s32[]{:S(2)}) async-start(), calls=%async_computation.21 | async-start | bytes 33554432 | tf_op jit(solution)/shard_map/psum | solution.py:182
  1627.9 1060.1 %all-reduce.97.cloned.1.call-start = ((), (), s32[]{:S(2)}) async-start(), calls=%async_computation.20 | async-start | bytes 2621440 | tf_op jit(solution)/shard_map/psum | solution.py:280
  1632.5 1362.5 %all-reduce.101.cloned.1.call-start = ((), (), s32[]{:S(2)}) async-start(), calls=%async_computation.22 | async-start | bytes 26738688 | tf_op jit(solution)/shard_map/psum | solution.py:276
  (98 other events, 585.6 us)
Sparse Core Ops, SparseCore 0:
  9.6 57.4 all-gather.6
  68.6 53.5 all-gather.8
  123.8 53.4 all-gather.10
  399.0 152.1 all-reduce.92
  552.6 115.4 all-gather.12
  669.6 113.5 all-gather.14
  784.7 113.5 all-gather.16
  937.3 151.0 all-reduce.94
  1110.5 93.9 reduce-scatter.10
  1342.3 93.8 reduce-scatter.6
  1568.9 93.1 reduce-scatter.8
  1664.3 212.3 reduce-scatter.12
  1879.1 212.8 reduce-scatter.14
  2094.2 212.8 reduce-scatter.16
  2309.7 289.3 all-reduce.98
  2603.6 84.3 all-reduce.96
  2690.8 304.0 all-reduce.100
where the time goes:
time: 3040 us; the launch traced here: 3020 us
  waiting for transfers between devices  1970 us (65%)
  local copies, waits for them, and re-layouts  565 us (19%)
  other arithmetic  203 us (7%)
  matrix products  194 us (6%)
  blocking collectives  56.9 us (2%)
    psum x1, waiting for transfers between devices, shards(): lax.psum((owned_branch, owned_input, owned_gate, owned_up, owned_out, own...  307 us
    psum x1, waiting for transfers between devices, shards(): output = (resid_rows + lax.psum(down_term, 'tp')).astype(jnp.bfloat16)  291 us
    reduce_scatter x1, waiting for transfers between devices, shards(): lax.psum_scatter(grad_w_up, 'fsdp', scatter_dimension=0, tiled=True)  215 us
    reduce_scatter x1, waiting for transfers between devices, shards(): lax.psum_scatter(grad_w_down, 'fsdp', scatter_dimension=1, tiled=True)  215 us
    reduce_scatter x1, waiting for transfers between devices, shards(): lax.psum_scatter(grad_w_gate, 'fsdp', scatter_dimension=0, tiled=True)  215 us
    slice x70, local copies, waits for them, and re-layouts, shards(): lax.associative_scan(linear_combine, (jnp.flip(next_factor, 1), jnp.flip(...  170 us
    psum x1, waiting for transfers between devices, shards(): grad_norm_mlp = lax.psum(mlp_back_term, 'tp')  151 us
    psum x1, waiting for transfers between devices, shards(): resid_rows = inputs + lax.psum(mixer_term, 'tp')  150 us
  transfers between devices with their start and end apart: 19, of which 15 were waited for; matrix products, arithmetic and copies ran while one was open for 29% of the time, Pallas kernels for 0%

commit v1 on v0

--- a/solution.py
+++ b/solution.py
@@ -179,7 +179,7 @@
     gate_act, gate_slope = gelu_slope(gate_pre)
     hidden = (gate_act * up_pre).astype(jnp.bfloat16)
     down_term = matmul(hidden, full_down)
-    output = (resid_rows + lax.psum(down_term, "tp")).astype(jnp.bfloat16)
+    output = (resid_rows + jnp.sum(lax.all_gather(down_term, "tp"), axis=0)).astype(jnp.bfloat16)
     grad_low = cotangent.reshape(row_count, model_width)
     grad_out = grad_low.astype(jnp.float32)
     grad_w_down = left_inner(hidden, grad_low)

time: 3040 us -> 2760 us (0.908)
  waiting for transfers between devices: 1970 us -> 1740 us
  local copies, waits for them, and re-layouts: 565 us -> 522 us
    reduce_scatter x1, waiting for transfers between devices: 215 us -> 0.02 us  [shards(): lax.psum_scatter(grad_w_up, 'fsdp', scatter_dimension=0, tiled=True)]
    reduce_scatter x1, waiting for transfers between devices: 215 us -> 0.02 us  [shards(): lax.psum_scatter(grad_w_gate, 'fsdp', scatter_dimension=0, tiled=True)]
    all_gather x0 -> x1, waiting for transfers between devices: none -> 196 us  [shards(): lax.all_gather(down_term, 'tp')]
    psum x1, waiting for transfers between devices: 291 us -> 155 us  [shards(): grad_norm_mix = lax.psum(mix_back_term, 'tp')]
    reduce_scatter x1, waiting for transfers between devices: 0.02 us -> 97.2 us  [shards(): lax.psum_scatter(grad_w_out, 'fsdp', scatter_dimension=1, tiled=True)]
    reduce_scatter x1, waiting for transfers between devices: 0.02 us -> 96.5 us  [shards(): lax.psum_scatter(grad_w_branch, 'fsdp', scatter_dimension=0, tiled=True)]
    reduce_scatter x1, waiting for transfers between devices: 215 us -> 131 us  [shards(): lax.psum_scatter(grad_w_down, 'fsdp', scatter_dimension=1, tiled=True)]
    reduce_scatter x1, waiting for transfers between devices: 29.5 us -> 96.5 us  [shards(): lax.psum_scatter(grad_w_input, 'fsdp', scatter_dimension=0, tiled=True)]
  transfers between devices with their start and end apart: 19 -> 20, of which waited for: 15 -> 16; matrix products, arithmetic and copies ran while one was open for 29% -> 31% of each run, Pallas kernels for 0% -> 0%
where the time goes in v1:
time: 2760 us; the launch traced here: 2740 us
  waiting for transfers between devices  1740 us (63%)
  local copies, waits for them, and re-layouts  522 us (19%)
  other arithmetic  203 us (7%)
  matrix products  193 us (7%)
  blocking collectives  56.8 us (2%)
    psum x1, waiting for transfers between devices, shards(): lax.psum((owned_branch, owned_input, owned_gate, owned_up, owned_out, own...  307 us
    all_gather x1, waiting for transfers between devices, shards(): lax.all_gather(down_term, 'tp')  196 us
    slice x70, local copies, waits for them, and re-layouts, shards(): lax.associative_scan(linear_combine, (jnp.flip(next_factor, 1), jnp.flip(...  171 us
    psum x1, waiting for transfers between devices, shards(): grad_norm_mix = lax.psum(mix_back_term, 'tp')  155 us
    psum x1, waiting for transfers between devices, shards(): resid_rows = inputs + lax.psum(mixer_term, 'tp')  150 us
    reduce_scatter x1, waiting for transfers between devices, shards(): lax.psum_scatter(grad_w_down, 'fsdp', scatter_dimension=1, tiled=True)  131 us
    slice x68, local copies, waits for them, and re-layouts, shards(): lax.associative_scan(linear_combine, (carry_factor, driven), axis=1)  130 us
    all_gather x1, waiting for transfers between devices, shards(): lax.all_gather(w_gate, 'fsdp', axis=0, tiled=True)  105 us
  transfers between devices with their start and end apart: 20, of which 16 were waited for; matrix products, arithmetic and copies ran while one was open for 31% of the time, Pallas kernels for 0%

profile of v1, /device:TPU:0, one launch (start us, length us, event | category | flops | bytes accessed | tf_op | source)
XLA Modules:
  0.0 2736.5 jit_solution(11645129124524112211)
XLA Ops:
  13.6 53.5 %all-gather.9.cloned.1.call-done = bf16[2048,640]{1,0:T(8,128)(2,1)} async-done(((bf16[512,640]{1,0:T(8,128)(2,1)}), bf16[2048,640]{1,0:T(8,128)(2,1)}) %all-gather.9.cloned.1.call-update) | async-done | bytes 2621456 | tf_op jit(solution)/shard_map/all_gather | solution.py:90
  67.1 6.5 convolution_convert_fusion
  93.8 6.6 fusion.65
  100.4 7.1 slice.691
  107.5 7.0 slice.692
  241.4 7.0 slice.762
  284.9 5.2 pad.269
  290.1 5.2 pad.270
  295.3 5.2 pad.289
  316.2 12.4 fusion.76
  328.6 7.8 fusion.138
  338.4 150.4 %all-reduce.92.cloned.1.call-done = f32[1024,2048]{1,0:T(8,128)} async-done(((f32[1024,2048]{1,0:T(8,128)}), f32[1024,2048]{1,0:T(8,128)}) %all-reduce.92.cloned.1.call-update) | async-done | bytes 8388624 | tf_op jit(solution)/shard_map/psum | solution.py:173
  488.8 5.7 multiply_reduce_fusion.2
  500.7 105.0 %all-gather.15.cloned.1.call-done = bf16[2048,1536]{1,0:T(8,128)(2,1)} async-done(((bf16[512,1536]{1,0:T(8,128)(2,1)}), bf16[2048,1536]{1,0:T(8,128)(2,1)}) %all-gather.15.cloned.1.call-update) | async-done | bytes 6291472 | tf_op jit(solution)/shard_map/all_gather | solution.py:91
  605.7 11.8 fusion.139
  617.6 103.1 %all-gather.17.cloned.1.call-done = bf16[2048,1536]{1,0:T(8,128)(2,1)} async-done(((bf16[512,1536]{1,0:T(8,128)(2,1)}), bf16[2048,1536]{1,0:T(8,128)(2,1)}) %all-gather.17.cloned.1.call-update) | async-done | bytes 6291472 | tf_op jit(solution)/shard_map/all_gather | solution.py:92
  720.7 11.7 fusion.140
  732.4 103.4 %all-gather.19.cloned.1.call-done = bf16[1536,2048]{1,0:T(8,128)(2,1)} async-done(((bf16[1536,512]{1,0:T(8,128)(2,1)}), bf16[1536,2048]{1,0:T(8,128)(2,1)}) %all-gather.19.cloned.1.call-update) | async-done | bytes 6291472 | tf_op jit(solution)/shard_map/all_gather | solution.py:94
  835.8 17.7 multiply_convert_fusion.1
  853.5 10.0 fusion.142
  863.6 10.9 convolution_add_fusion.1
  874.5 10.9 fusion.141
  885.5 12.6 fusion.145
  898.1 12.6 fusion.146
  910.8 12.2 fusion.30
  923.1 102.6 %all-reduce.94.cloned.1.call-done = f32[1024,2048]{1,0:T(8,128)} async-done(((f32[1024,2048]{1,0:T(8,128)}), f32[1024,2048]{1,0:T(8,128)}) %all-reduce.94.cloned.1.call-update) | async-done | bytes 8388624 | tf_op jit(solution)/shard_map/psum | solution.py:192
  1025.7 7.5 multiply_reduce_fusion
  1033.2 195.7 %all-gather.21.cloned.1.call-done = f32[4096,2048]{1,0:T(8,128)} async-done(((f32[1024,2048]{1,0:T(8,128)}), f32[4096,2048]{1,0:T(8,128)}) %all-gather.21.cloned.1.call-update) | async-done | bytes 33554448 | tf_op jit(solution)/shard_map/all_gather | solution.py:182
  1228.9 17.1 reduce_sum.137
  1246.0 13.1 multiply_add_fusion
  1270.7 7.1 slice.788
  1277.9 7.0 slice.793
  1284.9 7.0 slice.786
  1291.9 10.8 slice.789
  1302.6 10.7 slice.794
  1313.3 11.0 slice.787
  1324.3 12.7 fusion.54
  1337.1 20.7 reverse.9
  1357.8 7.0 slice.790
  1364.8 7.0 slice.791
  1484.1 7.0 slice.862
  1492.4 8.7 fusion.115
  1561.0 9.0 pad.330
  1584.7 9.0 pad.310
  1599.6 9.1 pad.309
  1611.2 9.0 pad.329
  1636.5 20.7 rev.13
  1657.2 20.9 rev.12
  1678.2 7.3 multiply_reduce_fusion.3
  1685.5 5.4 convert_reduce_fusion
  1703.1 8.8 fusion.44
  1721.0 5.6 fusion.27
  1726.9 5.4 fusion.89
  1732.3 5.9 convolution_add_fusion
  1742.9 130.6 %reduce-scatter.17.cloned.1.call-done = f32[1536,512]{1,0:T(8,128)} async-done(((f32[1536,2048]{1,0:T(8,128)}), f32[1536,512]{1,0:T(8,128)}) %reduce-scatter.17.cloned.1.call-update) | async-done | bytes 3145744 | tf_op jit(solution)/shard_map/reduce_scatter | solution.py:273
  1873.5 97.2 %reduce-scatter.11.cloned.1.call-done = f32[640,512]{1,0:T(8,128)} async-done(((f32[640,2048]{1,0:T(8,128)}), f32[640,512]{1,0:T(8,128)}) %reduce-scatter.11.cloned.1.call-update) | async-done | bytes 1310736 | tf_op jit(solution)/shard_map/reduce_scatter | solution.py:272
  1970.7 96.5 %reduce-scatter.7.cloned.1.call-done = f32[512,640]{1,0:T(8,128)} async-done(((f32[2048,640]{1,0:T(8,128)}), f32[512,640]{1,0:T(8,128)}) %reduce-scatter.7.cloned.1.call-update) | async-done | bytes 1310736 | tf_op jit(solution)/shard_map/reduce_scatter | solution.py:268
  2067.1 96.5 %reduce-scatter.9.cloned.1.call-done = f32[512,640]{1,0:T(8,128)} async-done(((f32[2048,640]{1,0:T(8,128)}), f32[512,640]{1,0:T(8,128)}) %reduce-scatter.9.cloned.1.call-update) | async-done | bytes 1310736 | tf_op jit(solution)/shard_map/reduce_scatter | solution.py:269
  2164.3 155.0 %all-reduce.96.cloned.1.call-done = f32[1024,2048]{1,0:T(8,128)} async-done(((f32[1024,2048]{1,0:T(8,128)}), f32[1024,2048]{1,0:T(8,128)}) %all-reduce.96.cloned.1.call-update) | async-done | bytes 8388624 | tf_op jit(solution)/shard_map/psum | solution.py:262
  2319.3 5.9 fusion.13
  2325.2 39.2 %all-reduce.83 = (f32[2048]{0:T(1024)}, f32[4,640]{1,0:T(4,128)}, f32[640]{0:T(1024)}, f32[640]{0:T(1024)}, f32[640]{0:T(1024)}, /*index=5*/f32[640]{0:T(1024)}, f32[2048]{0:T(1024)}) all-reduce(f32[2048]{0:T(1024)S(1)} %get-tuple-element.283, ...), channel_id=1, replica_groups=mesh['fsdp'=4,'ctx'=2,'tp'=4] {'fsdp','ctx'}, use_global_device_ids=true, to_apply=%region_13.14 | all-reduce | flops 9216 | bytes 73728 | tf_op jit(solution)/shard_map/psum | solution.py:280
  2364.4 10.3 fusion.29
  2374.8 33.6 %all-reduce.98.cloned.1.call-done = (f32[4,160,160]{2,1,0:T(8,128)}, f32[4,160,160]{2,1,0:T(8,128)}) async-done(((f32[4,160,160]{2,1,0:T(8,128)}, f32[4,160,160]{2,1,0:T(8,128)}), (f32[4,160,160]{2,1,0:T(8,128)}, f32[4,160,160]{2,1,0:T(8,128)})) %all-reduce.98.cloned.1.call-update) | async-done | bytes 819216 | tf_op jit(solution)/shard_map/psum | solution.py:280
  2408.4 307.0 %all-reduce.100.cloned.1.call-done = (f32[512,640]{1,0:T(8,128)}, f32[512,640]{1,0:T(8,128)}, f32[640,512]{1,0:T(8,128)}, f32[512,1536]{1,0:T(8,128)}, f32[512,1536]{1,0:T(8,128)}, /*index=5*/f32[1536,512]{1,0:T(8,128)}) async-done(((f32[512,640]{1,0:T(8,128)}, f32[512,640]{1,0:T(8,128)}, f32[640,512]{1,0:T(8,128)}, f32[512,1536]{1,0:T(8,128)}, f32[512,1536]{1,0:T(8,128)}, ...) | async-done | bytes 13369360 | tf_op jit(solution)/shard_map/psum | solution.py:276
  (665 shorter events, 478.0 us)
Async XLA Ops:
  7.2 79.0 %copy-start = (bf16[4,160,160]{2,1,0:T(8,128)(2,1)S(1)}, bf16[4,160,160]{2,1,0:T(8,128)(2,1)}, u32[]{:S(2)}) copy-start(bf16[4,160,160]{2,1,0:T(8,128)(2,1)} %param.30) | copy-start | bytes 614404
  7.2 59.9 %all-gather.9.cloned.1.call-start = ((), (), s32[]{:S(2)}) async-start(), calls=%async_computation.6 | async-start | bytes 3276800 | tf_op jit(solution)/shard_map/all_gather | solution.py:90
  7.9 308.2 %all-gather.11.cloned.1.call-start = ((), (), s32[]{:S(2)}) async-start(), calls=%async_computation.7 | async-start | bytes 3276800 | tf_op jit(solution)/shard_map/all_gather | solution.py:89
  8.7 58.4 %copy-start.79 = (f32[2048]{0:T(1024)S(1)}, f32[2048]{0:T(1024)}, u32[]{:S(2)}) copy-start(f32[2048]{0:T(1024)} %param.25) | copy-start | bytes 24580
  8.7 319.9 %all-gather.13.cloned.1.call-start = ((), (), s32[]{:S(2)}) async-start(), calls=%async_computation.8 | async-start | bytes 3276800 | tf_op jit(solution)/shard_map/all_gather | solution.py:93
  9.5 479.3 %all-reduce.92.cloned.1.call-start = ((), (), s32[]{:S(2)}) async-start(), calls=%async_computation.9 | async-start | bytes 16777216 | tf_op jit(solution)/shard_map/psum | solution.py:173
  12.6 303.6 %copy-start.76 = (f32[1024]{0:T(1024)}, f32[1024]{0:T(1024)S(1)}, u32[]{:S(2)}) copy-start(f32[1024]{0:T(1024)S(1)} %add_rsqrt_fusion.1) | copy-start | bytes 12292
  12.7 65.6 %copy-start.68 = (f32[640]{0:T(1024)}, f32[640]{0:T(1024)S(1)}, u32[]{:S(2)}) copy-start(f32[640]{0:T(1024)S(1)} %get-tuple-element.290) | copy-start | bytes 7684
  12.7 65.6 %copy-start.70 = (f32[640]{0:T(1024)}, f32[640]{0:T(1024)S(1)}, u32[]{:S(2)}) copy-start(f32[640]{0:T(1024)S(1)} %get-tuple-element.291) | copy-start | bytes 7684
  12.7 65.6 %copy-start.72 = (f32[640]{0:T(1024)}, f32[640]{0:T(1024)S(1)}, u32[]{:S(2)}) copy-start(f32[640]{0:T(1024)S(1)} %get-tuple-element.292) | copy-start | bytes 7684
  12.7 65.6 %copy-start.74 = (f32[640]{0:T(1024)}, f32[640]{0:T(1024)S(1)}, u32[]{:S(2)}) copy-start(f32[640]{0:T(1024)S(1)} %get-tuple-element.293) | copy-start | bytes 7684
  12.8 81.0 %copy-start.56 = (f32[640]{0:T(1024)}, f32[640]{0:T(1024)S(1)}, u32[]{:S(2)}) copy-start(f32[640]{0:T(1024)S(1)} %fusion.106) | copy-start | bytes 7684
  13.6 64.8 %copy-start.117 = (pred[1024]{0:T(1024)(128)(4,1)}, pred[1024]{0:T(1024)(128)(4,1)S(1)}, u32[]{:S(2)}) copy-start(pred[1024]{0:T(1024)(128)(4,1)S(1)} %get-tuple-element.295) | copy-start | bytes 3076
  13.6 64.8 %copy-start.119 = (pred[1024]{0:T(1024)(128)(4,1)}, pred[1024]{0:T(1024)(128)(4,1)S(1)}, u32[]{:S(2)}) copy-start(pred[1024]{0:T(1024)(128)(4,1)S(1)} %get-tuple-element.296) | copy-start | bytes 3076
  13.6 64.8 %copy-start.122 = (f32[640]{0:T(1024)S(1)}, f32[640]{0:T(1024)}, u32[]{:S(2)}) copy-start(f32[640]{0:T(1024)} %param.29) | copy-start | bytes 7684
  73.6 4.7 collective-permute-start
  77.0 16.8 copy-start.83
  100.4 14.1 copy-start.11
  237.1 14.1 copy-start.87
  300.5 15.7 copy-start.80
  336.4 269.3 %all-gather.15.cloned.1.call-start = ((), (), s32[]{:S(2)}) async-start(), calls=%async_computation.10 | async-start | bytes 7864320 | tf_op jit(solution)/shard_map/all_gather | solution.py:91
  337.0 383.7 %all-gather.17.cloned.1.call-start = ((), (), s32[]{:S(2)}) async-start(), calls=%async_computation.11 | async-start | bytes 7864320 | tf_op jit(solution)/shard_map/all_gather | solution.py:92
  337.6 498.2 %all-gather.19.cloned.1.call-start = ((), (), s32[]{:S(2)}) async-start(), calls=%async_computation.12 | async-start | bytes 7864320 | tf_op jit(solution)/shard_map/all_gather | solution.py:94
  338.4 159.6 %copy-start.59 = (f32[2048]{0:T(1024)S(1)}, f32[2048]{0:T(1024)}, u32[]{:S(2)}) copy-start(f32[2048]{0:T(1024)} %param.36) | copy-start | bytes 24580
  338.4 687.3 %all-reduce.94.cloned.1.call-start = ((), (), s32[]{:S(2)}) async-start(), calls=%async_computation.13 | async-start | bytes 16777216 | tf_op jit(solution)/shard_map/psum | solution.py:192
  874.4 354.5 %all-gather.21.cloned.1.call-start = ((), (), s32[]{:S(2)}) async-start(), calls=%async_computation.21 | async-start | bytes 41943040 | tf_op jit(solution)/shard_map/all_gather | solution.py:182
  885.4 857.4 %reduce-scatter.13.cloned.1.call-start = ((), (), s32[]{:S(2)}) async-start(), calls=%async_computation.18 | async-start | bytes 15728640 | tf_op jit(solution)/shard_map/reduce_scatter | solution.py:270
  898.1 844.8 %reduce-scatter.15.cloned.1.call-start = ((), (), s32[]{:S(2)}) async-start(), calls=%async_computation.19 | async-start | bytes 15728640 | tf_op jit(solution)/shard_map/reduce_scatter | solution.py:271
  910.7 962.8 %reduce-scatter.17.cloned.1.call-start = ((), (), s32[]{:S(2)}) async-start(), calls=%async_computation.20 | async-start | bytes 15728640 | tf_op jit(solution)/shard_map/reduce_scatter | solution.py:273
  923.0 1047.6 %reduce-scatter.11.cloned.1.call-start = ((), (), s32[]{:S(2)}) async-start(), calls=%async_computation.17 | async-start | bytes 6553600 | tf_op jit(solution)/shard_map/reduce_scatter | solution.py:272
  1246.0 16.4 copy-start.39
  1267.2 799.9 %reduce-scatter.7.cloned.1.call-start = ((), (), s32[]{:S(2)}) async-start(), calls=%async_computation.15 | async-start | bytes 6553600 | tf_op jit(solution)/shard_map/reduce_scatter | solution.py:268
  1472.8 19.1 copy-start.88
  1472.8 19.1 copy-start.89
  1472.8 19.1 copy-start.90
  1472.8 19.1 copy-start.91
  1472.8 19.2 copy-start.64
  1472.8 19.2 copy-start.65
  1472.8 19.4 copy-start.66
  1472.8 19.4 copy-start.67
  1472.8 19.4 copy-start.110
  1472.9 19.4 copy-start.109
  1477.2 15.2 copy-start.77
  1477.2 15.2 copy-start.81
  1501.1 662.5 %reduce-scatter.9.cloned.1.call-start = ((), (), s32[]{:S(2)}) async-start(), calls=%async_computation.16 | async-start | bytes 6553600 | tf_op jit(solution)/shard_map/reduce_scatter | solution.py:269
  1657.2 20.9 copy-start.5
  1657.2 20.9 copy-start.55
  1657.2 20.9 copy-start.57
  1657.2 20.9 copy-start.61
  1657.2 20.9 copy-start.63
  1657.2 20.9 copy-start.84
  1703.0 14.5 copy-start.69
  1703.0 14.5 copy-start.71
  1703.0 14.5 copy-start.73
  1703.0 14.5 copy-start.75
  1703.1 14.5 copy-start.123
  1703.1 14.5 copy-start.124
  1703.1 14.5 copy-start.125
  1703.1 17.9 copy-start.3
  1712.0 5.6 collective-permute-start.1
  1726.6 592.7 %all-reduce.96.cloned.1.call-start = ((), (), s32[]{:S(2)}) async-start(), calls=%async_computation.14 | async-start | bytes 16777216 | tf_op jit(solution)/shard_map/psum | solution.py:262
  1738.2 670.1 %all-reduce.98.cloned.1.call-start = ((), (), s32[]{:S(2)}) async-start(), calls=%async_computation.22 | async-start | bytes 2621440 | tf_op jit(solution)/shard_map/psum | solution.py:280
  1742.8 972.5 %all-reduce.100.cloned.1.call-start = ((), (), s32[]{:S(2)}) async-start(), calls=%async_computation.23 | async-start | bytes 26738688 | tf_op jit(solution)/shard_map/psum | solution.py:276
  2164.3 160.9 %copy-start.78 = (f32[2048]{0:T(1024)S(1)}, f32[2048]{0:T(1024)}, u32[]{:S(2)}) copy-start(f32[2048]{0:T(1024)} %get-tuple-element.281) | copy-start | bytes 24580
  (86 other events, 388.3 us)
Sparse Core Ops, SparseCore 0:
  9.6 57.4 all-gather.8
  68.6 53.5 all-gather.10
  123.8 53.4 all-gather.12
  336.6 152.2 all-reduce.91
  490.2 115.4 all-gather.14
  607.2 113.5 all-gather.16
  722.3 113.5 all-gather.18
  874.6 151.0 all-reduce.93
  1027.2 201.6 all-gather.20
  1231.1 211.8 reduce-scatter.12
  1445.4 212.9 reduce-scatter.14
  1660.6 212.8 reduce-scatter.16
  1875.8 94.8 reduce-scatter.10
  1972.8 94.2 reduce-scatter.6
  2069.3 94.2 reduce-scatter.8
  2165.9 153.3 all-reduce.95
  2323.9 84.3 all-reduce.97
  2411.2 304.0 all-reduce.99
